TPU v7x, 512 devices: a whole 4x8x8 slice. The times are simulated.
512 devices in a mesh: seq: 16 (over y_hi, z), head: 32 (over x, y_lo, core).
Axes of the slice: x: 4, y: 8 (y_hi: 2, y_lo: 4; y = y_hi * 4 + y_lo), z: 8, core: 2. Of those that a mesh axis runs over, the one named last changes fastest.
Arguments:
- tokens: bfloat16 [16384, 4096], P(('seq', 'head')), may hold values from -6 to 6
- doc_lengths: int32 [16], replicated, may hold values from 1 to 8704, as said below
- value_weight: bfloat16 [4096, 8192], P('seq', 'head'), may hold values from -0.09375 to 0.09375
- gate_weight: bfloat16 [4096, 8192], P('seq', 'head'), may hold values from -0.09375 to 0.09375
- state_weight: bfloat16 [8, 4096, 256], P(None, 'seq'), may hold values from -0.09375 to 0.09375
- step_weight: bfloat16 [4096, 128], P('seq', 'head'), may hold values from -0.09375 to 0.09375
- value_conv: float32 [4, 8192], P(None, 'head'), may hold values from -3 to 3
- state_conv: float32 [8, 4, 256], replicated, may hold values from -3 to 3
- step_bias: float32 [128], P('head'), may hold values from -5 to -3
- log_rate: float32 [128], P('head'), may hold values from -6 to 4
Outputs:
- layer_output: bfloat16 [16384, 8192], P('seq', 'head')
Inputs may be any that keep to these rules, and one draw needn't show every extreme that they name: `doc_lengths`: the 16 documents lie one after another, their lengths sum to 16384, and the last one holds 8704 positions.
All inputs are finite; a program needn't handle non-finite values.
Results may differ from a plain program's by a relative error of at most 0.015.
Values may be sent and summed in bfloat16 or wider, within the bound.
No kernel may reach another device: no remote copies, remote signals or barrier semaphores. Data moves between devices by JAX's collectives and lax.ppermute only.
A program may use at most 64 MiB of HBM per device.

v0:
```python
import jax
import jax.numpy as jnp
from jax import lax
from jax.sharding import PartitionSpec as P

HEADS = 128
GROUPS = 8
BLOCK = 256


def passed_along(value, axis, steps):
    count = lax.axis_size(axis)
    leading, last = (max(0, -steps), min(count, count - steps))
    return lax.ppermute(value, axis, [(source, source + steps) for source in range(leading, last)])


def segment_of(positions, starts):
    reached = (starts[None, :] <= positions[:, None]).astype(jnp.int32)
    return jnp.sum(reached, axis=1) - 1


def causal_conv(extended, taps_weight, seg_ext, row_count):
    tap_count = taps_weight.shape[0]
    own_segment = seg_ext[tap_count - 1 :]
    summed = jnp.zeros((row_count, extended.shape[1]), jnp.float32)
    for tap_index in range(tap_count):
        window = extended[tap_index : tap_index + row_count].astype(jnp.float32)
        keep_mask = (seg_ext[tap_index : tap_index + row_count] == own_segment).astype(jnp.float32)[
            :, None
        ]
        summed = summed + taps_weight[tap_index][None, :] * window * keep_mask
    return jax.nn.silu(summed).astype(jnp.bfloat16)


def block_terms(b_rows, c_rows, x_rows, decay_rows, step_rows, segments, seg_before):
    block_len = b_rows.shape[0]
    head_total = decay_rows.shape[0]
    x_heads = x_rows.reshape(block_len, head_total, -1)
    cumulative = jnp.cumsum(decay_rows, axis=1)
    products = jnp.dot(c_rows, b_rows.T, preferred_element_type=jnp.float32)
    local_index = jnp.arange(block_len)
    allowed = (local_index[None, :] <= local_index[:, None]) & (
        segments[None, :] == segments[:, None]
    )
    spread = cumulative[:, :, None] - cumulative[:, None, :]
    decay_mat = jnp.where(allowed[None], jnp.exp(jnp.where(allowed[None], spread, 0.0)), 0.0)
    scores = (products[None] * decay_mat * step_rows[:, None, :]).astype(jnp.bfloat16)
    y_inner = jnp.einsum("hij,jhp->ihp", scores, x_heads, preferred_element_type=jnp.float32)
    ending = cumulative[:, -1]
    trailing = (
        jnp.where((segments == segments[-1])[None, :], jnp.exp(ending[:, None] - cumulative), 0.0)
        * step_rows
    )
    weighted = (trailing.T[:, :, None] * x_heads.astype(jnp.float32)).astype(jnp.bfloat16)
    local_state = jnp.einsum("jn,jhp->hnp", b_rows, weighted, preferred_element_type=jnp.float32)
    factor = jnp.where(segments[-1] == seg_before, jnp.exp(ending), 0.0)
    entry_gain = jnp.where((segments == seg_before)[None, :], jnp.exp(cumulative), 0.0)
    return (y_inner.reshape(block_len, -1), local_state, factor, entry_gain)


def local_pass(state_cols, value_cols, decay_cols, step_cols, seg_rows, seg_before, block_len):
    block_count = state_cols.shape[0] // block_len
    state_dim = state_cols.shape[1] // 2
    head_total = decay_cols.shape[1]
    b_all = state_cols[:, :state_dim].reshape(block_count, block_len, state_dim)
    c_all = state_cols[:, state_dim:].reshape(block_count, block_len, state_dim)
    x_all = value_cols.reshape(block_count, block_len, -1)
    decay_all = decay_cols.reshape(block_count, block_len, head_total).transpose(0, 2, 1)
    step_all = step_cols.reshape(block_count, block_len, head_total).transpose(0, 2, 1)
    seg_all = seg_rows.reshape(block_count, block_len)

    def one_block(block_item):
        return block_terms(*block_item)

    outputs = lax.map(one_block, (b_all, c_all, x_all, decay_all, step_all, seg_all, seg_before))
    return (outputs, c_all)


def prefix_blocks(local_state, factor):

    def chain_step(carry_pair, block_item):
        running, running_gain = carry_pair
        local_term, factor_term = block_item
        return (
            (factor_term[:, None, None] * running + local_term, factor_term * running_gain),
            (running, running_gain),
        )

    initial = (
        jnp.zeros(local_state.shape[1:], jnp.float32),
        jnp.ones((factor.shape[1],), jnp.float32),
    )
    (shard_state, shard_gain), (inside, gain_list) = lax.scan(
        chain_step, initial, (local_state, factor)
    )
    return (shard_state, shard_gain, inside, gain_list)


def finish(y_inner, incoming, entry_gain, c_all, value_cols, gate_cols):
    block_count, block_len, _ = y_inner.shape
    head_total = incoming.shape[1]
    carried = jnp.einsum(
        "cin,chnp->cihp", c_all.astype(jnp.float32), incoming, precision=lax.Precision.HIGHEST
    )
    carried = carried * entry_gain.transpose(0, 2, 1)[:, :, :, None]
    x_heads = value_cols.reshape(block_count, block_len, head_total, -1).astype(jnp.float32)
    summed = y_inner.reshape(block_count, block_len, head_total, -1) + carried + x_heads
    gating = jax.nn.silu(gate_cols.astype(jnp.float32)).reshape(
        block_count, block_len, head_total, -1
    )
    return (summed * gating).reshape(block_count * block_len, -1).astype(jnp.bfloat16)


def local(
    tokens,
    doc_lengths,
    value_weight,
    gate_weight,
    state_weight,
    step_weight,
    value_conv,
    state_conv,
    step_bias,
    log_rate,
):
    tok_dev = tokens.shape[0] * lax.axis_size("head")
    heads_here = step_weight.shape[1]
    tap_count = value_conv.shape[0]
    group_index = lax.axis_index("head") * heads_here // (HEADS // GROUPS)
    state_own = lax.dynamic_index_in_dim(state_weight, group_index, 0, keepdims=False)
    conv_own = lax.dynamic_index_in_dim(state_conv, group_index, 0, keepdims=False)
    gathered = lax.all_gather(tokens, "head", axis=0, tiled=True)
    shard_pieces = (
        lax.all_gather(value_weight, "seq", axis=0, tiled=True),
        lax.all_gather(gate_weight, "seq", axis=0, tiled=True),
        lax.all_gather(state_own, "seq", axis=0, tiled=True),
        lax.all_gather(step_weight, "seq", axis=0, tiled=True),
    )
    projected = tuple(
        (
            jnp.dot(gathered, weight_piece, preferred_element_type=jnp.float32)
            for weight_piece in shard_pieces
        )
    )
    value_proj = projected[0].astype(jnp.bfloat16)
    gate_proj = projected[1].astype(jnp.bfloat16)
    state_proj = projected[2].astype(jnp.bfloat16)
    step_proj = projected[3].astype(jnp.bfloat16)
    value_cols = value_proj.shape[1]
    rim_source = jnp.concatenate(
        [value_proj[-(tap_count - 1) :], state_proj[-(tap_count - 1) :]], axis=1
    )
    rim_rows = passed_along(rim_source, "seq", 1)
    value_ext = jnp.concatenate([rim_rows[:, :value_cols], value_proj], axis=0)
    state_ext = jnp.concatenate([rim_rows[:, value_cols:], state_proj], axis=0)
    starts = jnp.cumsum(doc_lengths) - doc_lengths
    positions = lax.axis_index("seq") * tok_dev + jnp.arange(-(tap_count - 1), tok_dev)
    seg_ext = segment_of(positions, starts)
    value_act = causal_conv(value_ext, value_conv, seg_ext, tok_dev)
    state_act = causal_conv(state_ext, conv_own, seg_ext, tok_dev)
    step_size = jax.nn.softplus(step_proj.astype(jnp.float32) + step_bias[None, :])
    decay_rate = -jnp.exp(log_rate)[None, :] * step_size
    seg_rows = seg_ext[tap_count - 1 :]
    seg_before = seg_ext[tap_count - 2 : tap_count - 2 + tok_dev : BLOCK]
    (y_inner, local_state, factor, entry_gain), c_all = local_pass(
        state_act, value_act, decay_rate, step_size, seg_rows, seg_before, BLOCK
    )
    shard_state, shard_gain, inside, gain_list = prefix_blocks(local_state, factor)

    def relay(step_index, arriving):
        leaving = shard_gain[:, None, None] * arriving + shard_state
        return passed_along(leaving, "seq", 1)

    entering = lax.fori_loop(0, lax.axis_size("seq") - 1, relay, jnp.zeros_like(shard_state))
    incoming = inside + gain_list[:, :, None, None] * entering[None]
    return finish(y_inner, incoming, entry_gain, c_all, value_act, gate_proj)


def solution(mesh):
    return jax.shard_map(
        local,
        mesh=mesh,
        in_specs=(
            P(("seq", "head"), None),
            P(),
            P("seq", "head"),
            P("seq", "head"),
            P(None, "seq", None),
            P("seq", "head"),
            P(None, "head"),
            P(),
            P("head"),
            P("head"),
        ),
        out_specs=P("seq", "head"),
        check_vma=False,
    )
```

profile of v0, /device:TPU:48, one launch (start us, length us, event | category | flops | bytes accessed | tf_op | source)
XLA Modules:
  0.0 720.9 jit_solution(3404737921538199455)
XLA Ops:
  11.2 56.0 %all_gather.18 = bf16[4096,4]{0,1:T(4,128)(2,1)S(1)} all-gather(bf16[256,4]{0,1:T(4,128)(2,1)} %param.21), channel_id=1, replica_groups=mesh['seq'=16,'head'=32] {'seq'}, dimensions={0}, use_global_device_ids=true | all-gather | bytes 34816 | tf_op jit(solution)/shard_map/all_gather | solution.py:137
  69.7 48.0 %all-gather.8.cloned.1.call-done = bf16[4096,256]{1,0:T(8,128)(2,1)} async-done(((bf16[256,256]{1,0:T(8,128)(2,1)}), bf16[4096,256]{1,0:T(8,128)(2,1)}) %all-gather.8.cloned.1.call-update) | async-done | bytes 2097168 | tf_op jit(solution)/shard_map/all_gather | solution.py:134
  117.7 69.9 %all-gather.6.cloned.1.call-done = bf16[1024,4096]{1,0:T(8,128)(2,1)} async-done(((bf16[32,4096]{1,0:T(8,128)(2,1)}), bf16[1024,4096]{1,0:T(8,128)(2,1)}) %all-gather.6.cloned.1.call-update) | async-done | bytes 8388624 | tf_op jit(solution)/shard_map/all_gather | solution.py:132
  187.6 6.3 convolution_convert_fusion.1
  194.7 98.4 %all-gather.12.cloned.1.call-done = bf16[1,4096,256]{2,1,0:T(8,128)(2,1)} async-done(((bf16[1,256,256]{2,1,0:T(8,128)(2,1)}), bf16[1,4096,256]{2,1,0:T(8,128)(2,1)}) %all-gather.12.cloned.1.call-update) | async-done | bytes 2097168 | tf_op jit(solution)/shard_map/all_gather | solution.py:136
  303.3 92.2 %all-gather.10.cloned.1.call-done = bf16[4096,256]{1,0:T(8,128)(2,1)} async-done(((bf16[256,256]{1,0:T(8,128)(2,1)}), bf16[4096,256]{1,0:T(8,128)(2,1)}) %all-gather.10.cloned.1.call-update) | async-done | bytes 2097168 | tf_op jit(solution)/shard_map/all_gather | solution.py:135
  395.5 7.4 %convert_multiply_fusion = f32[1024,256]{1,0:T(8,128)} fusion(bf16[1024,4096]{1,0:T(8,128)(2,1)} %all-gather.6.cloned.1.call-done, bf16[4096,256]{1,0:T(8,128)(2,1)} %all-gather.10.cloned.1.call-done), kind=kOutput, calls=%fused_computation.49 | convolution fusion | flops 2149056512 | bytes 11534336 | tf_op jit(solution)/shard_map/dot_general | solution.py:141
  418.4 30.8 %while.43 = (s32[]{:T(128)}, f32[4,256,256]{1,2,0:T(8,128)}, f32[4,4,128,64]{2,3,1,0:T(8,128)S(1)}, f32[4,4]{1,0:T(4,128)S(1)}, f32[4,4,256]{2,1,0:T(4,128)S(1)}...) while((s32[]{:T(128)}, f32[4,256,256]{1,2,0:T(8,128)}, ...), condition=%wide.region_5.6_spmd, body=%wide.region_2.5_spmd.sunk | while | flops 69210640 | bytes 2915319 | solution.py:75
  454.1 247.6 %while.44 = (s32[]{:T(128)}, f32[4,128,64]{2,1,0:T(8,128)S(1)}, f32[4]{0:T(128)S(1)}, f32[4,128,64]{2,1,0:T(8,128)S(1)}, s32[]{:T(128)}) while((s32[]{:T(128)}, f32[4,128,64]{2,1,0:T(8,128)S(1)}, f32[4]{0:T(128)S(1)}, f32[4,128,64]{2,1,0:T(8,128)S(1)}, s32[]{:T(128)}) %tuple.85), condition=%wide.region_9.10_spmd, body=%wide.region_8.9_spmd.sunk | while | flops 65538 | bytes 917621 | solution.py:174
  457.2 12.6 %collective-permute-done = f32[4,128,64]{2,1,0:T(8,128)S(1)} collective-permute-done((f32[4,128,64]{2,1,0:T(8,128)S(1)}, f32[4,128,64]{2,1,0:T(8,128)S(1)}, u32[]{:S(2)}, u32[]{:S(2)}) %collective-permute-start) | collective-permute-done | bytes 131104 | tf_op jit(solution)/shard_map/while/body/eval_jaxpr/ppermute | solution.py:14
  471.8 15.3 %collective-permute-done = f32[4,128,64]{2,1,0:T(8,128)S(1)} collective-permute-done((f32[4,128,64]{2,1,0:T(8,128)S(1)}, f32[4,128,64]{2,1,0:T(8,128)S(1)}, u32[]{:S(2)}, u32[]{:S(2)}) %collective-permute-start) | collective-permute-done | bytes 131104 | tf_op jit(solution)/shard_map/while/body/eval_jaxpr/ppermute | solution.py:14
  489.1 15.1 %collective-permute-done = f32[4,128,64]{2,1,0:T(8,128)S(1)} collective-permute-done((f32[4,128,64]{2,1,0:T(8,128)S(1)}, f32[4,128,64]{2,1,0:T(8,128)S(1)}, u32[]{:S(2)}, u32[]{:S(2)}) %collective-permute-start) | collective-permute-done | bytes 131104 | tf_op jit(solution)/shard_map/while/body/eval_jaxpr/ppermute | solution.py:14
  506.2 15.1 %collective-permute-done = f32[4,128,64]{2,1,0:T(8,128)S(1)} collective-permute-done((f32[4,128,64]{2,1,0:T(8,128)S(1)}, f32[4,128,64]{2,1,0:T(8,128)S(1)}, u32[]{:S(2)}, u32[]{:S(2)}) %collective-permute-start) | collective-permute-done | bytes 131104 | tf_op jit(solution)/shard_map/while/body/eval_jaxpr/ppermute | solution.py:14
  523.3 19.9 %collective-permute-done = f32[4,128,64]{2,1,0:T(8,128)S(1)} collective-permute-done((f32[4,128,64]{2,1,0:T(8,128)S(1)}, f32[4,128,64]{2,1,0:T(8,128)S(1)}, u32[]{:S(2)}, u32[]{:S(2)}) %collective-permute-start) | collective-permute-done | bytes 131104 | tf_op jit(solution)/shard_map/while/body/eval_jaxpr/ppermute | solution.py:14
  545.2 17.7 %collective-permute-done = f32[4,128,64]{2,1,0:T(8,128)S(1)} collective-permute-done((f32[4,128,64]{2,1,0:T(8,128)S(1)}, f32[4,128,64]{2,1,0:T(8,128)S(1)}, u32[]{:S(2)}, u32[]{:S(2)}) %collective-permute-start) | collective-permute-done | bytes 131104 | tf_op jit(solution)/shard_map/while/body/eval_jaxpr/ppermute | solution.py:14
  564.9 15.2 %collective-permute-done = f32[4,128,64]{2,1,0:T(8,128)S(1)} collective-permute-done((f32[4,128,64]{2,1,0:T(8,128)S(1)}, f32[4,128,64]{2,1,0:T(8,128)S(1)}, u32[]{:S(2)}, u32[]{:S(2)}) %collective-permute-start) | collective-permute-done | bytes 131104 | tf_op jit(solution)/shard_map/while/body/eval_jaxpr/ppermute | solution.py:14
  582.1 14.3 %collective-permute-done = f32[4,128,64]{2,1,0:T(8,128)S(1)} collective-permute-done((f32[4,128,64]{2,1,0:T(8,128)S(1)}, f32[4,128,64]{2,1,0:T(8,128)S(1)}, u32[]{:S(2)}, u32[]{:S(2)}) %collective-permute-start) | collective-permute-done | bytes 131104 | tf_op jit(solution)/shard_map/while/body/eval_jaxpr/ppermute | solution.py:14
  598.4 16.3 %collective-permute-done = f32[4,128,64]{2,1,0:T(8,128)S(1)} collective-permute-done((f32[4,128,64]{2,1,0:T(8,128)S(1)}, f32[4,128,64]{2,1,0:T(8,128)S(1)}, u32[]{:S(2)}, u32[]{:S(2)}) %collective-permute-start) | collective-permute-done | bytes 131104 | tf_op jit(solution)/shard_map/while/body/eval_jaxpr/ppermute | solution.py:14
  616.8 13.1 %collective-permute-done = f32[4,128,64]{2,1,0:T(8,128)S(1)} collective-permute-done((f32[4,128,64]{2,1,0:T(8,128)S(1)}, f32[4,128,64]{2,1,0:T(8,128)S(1)}, u32[]{:S(2)}, u32[]{:S(2)}) %collective-permute-start) | collective-permute-done | bytes 131104 | tf_op jit(solution)/shard_map/while/body/eval_jaxpr/ppermute | solution.py:14
  631.9 12.4 %collective-permute-done = f32[4,128,64]{2,1,0:T(8,128)S(1)} collective-permute-done((f32[4,128,64]{2,1,0:T(8,128)S(1)}, f32[4,128,64]{2,1,0:T(8,128)S(1)}, u32[]{:S(2)}, u32[]{:S(2)}) %collective-permute-start) | collective-permute-done | bytes 131104 | tf_op jit(solution)/shard_map/while/body/eval_jaxpr/ppermute | solution.py:14
  646.3 12.4 %collective-permute-done = f32[4,128,64]{2,1,0:T(8,128)S(1)} collective-permute-done((f32[4,128,64]{2,1,0:T(8,128)S(1)}, f32[4,128,64]{2,1,0:T(8,128)S(1)}, u32[]{:S(2)}, u32[]{:S(2)}) %collective-permute-start) | collective-permute-done | bytes 131104 | tf_op jit(solution)/shard_map/while/body/eval_jaxpr/ppermute | solution.py:14
  660.6 12.4 %collective-permute-done = f32[4,128,64]{2,1,0:T(8,128)S(1)} collective-permute-done((f32[4,128,64]{2,1,0:T(8,128)S(1)}, f32[4,128,64]{2,1,0:T(8,128)S(1)}, u32[]{:S(2)}, u32[]{:S(2)}) %collective-permute-start) | collective-permute-done | bytes 131104 | tf_op jit(solution)/shard_map/while/body/eval_jaxpr/ppermute | solution.py:14
  675.0 12.4 %collective-permute-done = f32[4,128,64]{2,1,0:T(8,128)S(1)} collective-permute-done((f32[4,128,64]{2,1,0:T(8,128)S(1)}, f32[4,128,64]{2,1,0:T(8,128)S(1)}, u32[]{:S(2)}, u32[]{:S(2)}) %collective-permute-start) | collective-permute-done | bytes 131104 | tf_op jit(solution)/shard_map/while/body/eval_jaxpr/ppermute | solution.py:14
  689.4 12.4 %collective-permute-done = f32[4,128,64]{2,1,0:T(8,128)S(1)} collective-permute-done((f32[4,128,64]{2,1,0:T(8,128)S(1)}, f32[4,128,64]{2,1,0:T(8,128)S(1)}, u32[]{:S(2)}, u32[]{:S(2)}) %collective-permute-start) | collective-permute-done | bytes 131104 | tf_op jit(solution)/shard_map/while/body/eval_jaxpr/ppermute | solution.py:14
  (240 shorter events, 111.6 us)
Async XLA Ops:
  6.5 111.1 %all-gather.8.cloned.1.call-start = ((), (), s32[]{:S(2)}) async-start(), calls=%async_computation.1 | async-start | bytes 2228224 | tf_op jit(solution)/shard_map/all_gather | solution.py:134
  7.3 180.3 %all-gather.6.cloned.1.call-start = ((), (), s32[]{:S(2)}) async-start(), calls=%async_computation | async-start | bytes 8650752 | tf_op jit(solution)/shard_map/all_gather | solution.py:132
  8.0 285.1 %all-gather.12.cloned.1.call-start = ((), (), s32[]{:S(2)}) async-start(), calls=%async_computation.3 | async-start | bytes 2228224 | tf_op jit(solution)/shard_map/all_gather | solution.py:136
  8.8 386.7 %all-gather.10.cloned.1.call-start = ((), (), s32[]{:S(2)}) async-start(), calls=%async_computation.2 | async-start | bytes 2228224 | tf_op jit(solution)/shard_map/all_gather | solution.py:135
  300.2 102.6 %copy-start.9 = (f32[4]{0:T(128)S(1)}, f32[4]{0:T(128)}, u32[]{:S(2)}) copy-start(f32[4]{0:T(128)} %param.24) | copy-start | bytes 52
  300.3 112.0 %collective-permute-start.1 = (bf16[3,512]{1,0:T(4,128)(2,1)S(1)}, bf16[3,512]{1,0:T(4,128)(2,1)S(1)}, u32[]{:S(2)}, u32[]{:S(2)}) collective-permute-start(bf16[3,512]{1,0:T(4,128)(2,1)S(1)} %pad_maximum_fusion.2), channel_id=1, source_target_pairs={{0,32},{32,64},{64,96},{96,128},{128,160},{160,192},{192,224},{224... | collective-permute-start | bytes 9224 | tf_op jit(solution)/shard_map/ppermute | solution.py:14
  454.1 247.7 %copy-start.4 = (f32[4,4,128,64]{3,2,1,0:T(8,128)S(1)}, f32[4,4,128,64]{3,2,1,0:T(8,128)}, u32[]{:S(2)}) copy-start(f32[4,4,128,64]{3,2,1,0:T(8,128)} %get-tuple-element.135) | copy-start | bytes 1572868
  454.2 15.5 %collective-permute-start = (f32[4,128,64]{2,1,0:T(8,128)S(1)}, f32[4,128,64]{2,1,0:T(8,128)S(1)}, u32[]{:S(2)}, u32[]{:S(2)}) collective-permute-start(f32[4,128,64]{2,1,0:T(8,128)S(1)} %multiply_add_fusion.3), channel_id=1, source_target_pairs={{0,32},{32,64},{64,96},{96,128},{128,160},{160,192},{192,224},{224... | collective-permute-start | bytes 393224 | tf_op jit(solution)/shard_map/while/body/eval_jaxpr/ppermute | solution.py:14
  469.9 17.2 %collective-permute-start = (f32[4,128,64]{2,1,0:T(8,128)S(1)}, f32[4,128,64]{2,1,0:T(8,128)S(1)}, u32[]{:S(2)}, u32[]{:S(2)}) collective-permute-start(f32[4,128,64]{2,1,0:T(8,128)S(1)} %multiply_add_fusion.3), channel_id=1, source_target_pairs={{0,32},{32,64},{64,96},{96,128},{128,160},{160,192},{192,224},{224... | collective-permute-start | bytes 393224 | tf_op jit(solution)/shard_map/while/body/eval_jaxpr/ppermute | solution.py:14
  487.2 17.0 %collective-permute-start = (f32[4,128,64]{2,1,0:T(8,128)S(1)}, f32[4,128,64]{2,1,0:T(8,128)S(1)}, u32[]{:S(2)}, u32[]{:S(2)}) collective-permute-start(f32[4,128,64]{2,1,0:T(8,128)S(1)} %multiply_add_fusion.3), channel_id=1, source_target_pairs={{0,32},{32,64},{64,96},{96,128},{128,160},{160,192},{192,224},{224... | collective-permute-start | bytes 393224 | tf_op jit(solution)/shard_map/while/body/eval_jaxpr/ppermute | solution.py:14
  504.3 17.0 %collective-permute-start = (f32[4,128,64]{2,1,0:T(8,128)S(1)}, f32[4,128,64]{2,1,0:T(8,128)S(1)}, u32[]{:S(2)}, u32[]{:S(2)}) collective-permute-start(f32[4,128,64]{2,1,0:T(8,128)S(1)} %multiply_add_fusion.3), channel_id=1, source_target_pairs={{0,32},{32,64},{64,96},{96,128},{128,160},{160,192},{192,224},{224... | collective-permute-start | bytes 393224 | tf_op jit(solution)/shard_map/while/body/eval_jaxpr/ppermute | solution.py:14
  521.4 21.8 %collective-permute-start = (f32[4,128,64]{2,1,0:T(8,128)S(1)}, f32[4,128,64]{2,1,0:T(8,128)S(1)}, u32[]{:S(2)}, u32[]{:S(2)}) collective-permute-start(f32[4,128,64]{2,1,0:T(8,128)S(1)} %multiply_add_fusion.3), channel_id=1, source_target_pairs={{0,32},{32,64},{64,96},{96,128},{128,160},{160,192},{192,224},{224... | collective-permute-start | bytes 393224 | tf_op jit(solution)/shard_map/while/body/eval_jaxpr/ppermute | solution.py:14
  543.3 19.6 %collective-permute-start = (f32[4,128,64]{2,1,0:T(8,128)S(1)}, f32[4,128,64]{2,1,0:T(8,128)S(1)}, u32[]{:S(2)}, u32[]{:S(2)}) collective-permute-start(f32[4,128,64]{2,1,0:T(8,128)S(1)} %multiply_add_fusion.3), channel_id=1, source_target_pairs={{0,32},{32,64},{64,96},{96,128},{128,160},{160,192},{192,224},{224... | collective-permute-start | bytes 393224 | tf_op jit(solution)/shard_map/while/body/eval_jaxpr/ppermute | solution.py:14
  563.0 17.1 %collective-permute-start = (f32[4,128,64]{2,1,0:T(8,128)S(1)}, f32[4,128,64]{2,1,0:T(8,128)S(1)}, u32[]{:S(2)}, u32[]{:S(2)}) collective-permute-start(f32[4,128,64]{2,1,0:T(8,128)S(1)} %multiply_add_fusion.3), channel_id=1, source_target_pairs={{0,32},{32,64},{64,96},{96,128},{128,160},{160,192},{192,224},{224... | collective-permute-start | bytes 393224 | tf_op jit(solution)/shard_map/while/body/eval_jaxpr/ppermute | solution.py:14
  580.2 16.2 %collective-permute-start = (f32[4,128,64]{2,1,0:T(8,128)S(1)}, f32[4,128,64]{2,1,0:T(8,128)S(1)}, u32[]{:S(2)}, u32[]{:S(2)}) collective-permute-start(f32[4,128,64]{2,1,0:T(8,128)S(1)} %multiply_add_fusion.3), channel_id=1, source_target_pairs={{0,32},{32,64},{64,96},{96,128},{128,160},{160,192},{192,224},{224... | collective-permute-start | bytes 393224 | tf_op jit(solution)/shard_map/while/body/eval_jaxpr/ppermute | solution.py:14
  596.5 18.2 %collective-permute-start = (f32[4,128,64]{2,1,0:T(8,128)S(1)}, f32[4,128,64]{2,1,0:T(8,128)S(1)}, u32[]{:S(2)}, u32[]{:S(2)}) collective-permute-start(f32[4,128,64]{2,1,0:T(8,128)S(1)} %multiply_add_fusion.3), channel_id=1, source_target_pairs={{0,32},{32,64},{64,96},{96,128},{128,160},{160,192},{192,224},{224... | collective-permute-start | bytes 393224 | tf_op jit(solution)/shard_map/while/body/eval_jaxpr/ppermute | solution.py:14
  614.8 15.0 %collective-permute-start = (f32[4,128,64]{2,1,0:T(8,128)S(1)}, f32[4,128,64]{2,1,0:T(8,128)S(1)}, u32[]{:S(2)}, u32[]{:S(2)}) collective-permute-start(f32[4,128,64]{2,1,0:T(8,128)S(1)} %multiply_add_fusion.3), channel_id=1, source_target_pairs={{0,32},{32,64},{64,96},{96,128},{128,160},{160,192},{192,224},{224... | collective-permute-start | bytes 393224 | tf_op jit(solution)/shard_map/while/body/eval_jaxpr/ppermute | solution.py:14
  629.9 14.3 %collective-permute-start = (f32[4,128,64]{2,1,0:T(8,128)S(1)}, f32[4,128,64]{2,1,0:T(8,128)S(1)}, u32[]{:S(2)}, u32[]{:S(2)}) collective-permute-start(f32[4,128,64]{2,1,0:T(8,128)S(1)} %multiply_add_fusion.3), channel_id=1, source_target_pairs={{0,32},{32,64},{64,96},{96,128},{128,160},{160,192},{192,224},{224... | collective-permute-start | bytes 393224 | tf_op jit(solution)/shard_map/while/body/eval_jaxpr/ppermute | solution.py:14
  644.3 14.3 %collective-permute-start = (f32[4,128,64]{2,1,0:T(8,128)S(1)}, f32[4,128,64]{2,1,0:T(8,128)S(1)}, u32[]{:S(2)}, u32[]{:S(2)}) collective-permute-start(f32[4,128,64]{2,1,0:T(8,128)S(1)} %multiply_add_fusion.3), channel_id=1, source_target_pairs={{0,32},{32,64},{64,96},{96,128},{128,160},{160,192},{192,224},{224... | collective-permute-start | bytes 393224 | tf_op jit(solution)/shard_map/while/body/eval_jaxpr/ppermute | solution.py:14
  658.7 14.3 %collective-permute-start = (f32[4,128,64]{2,1,0:T(8,128)S(1)}, f32[4,128,64]{2,1,0:T(8,128)S(1)}, u32[]{:S(2)}, u32[]{:S(2)}) collective-permute-start(f32[4,128,64]{2,1,0:T(8,128)S(1)} %multiply_add_fusion.3), channel_id=1, source_target_pairs={{0,32},{32,64},{64,96},{96,128},{128,160},{160,192},{192,224},{224... | collective-permute-start | bytes 393224 | tf_op jit(solution)/shard_map/while/body/eval_jaxpr/ppermute | solution.py:14
  673.1 14.3 %collective-permute-start = (f32[4,128,64]{2,1,0:T(8,128)S(1)}, f32[4,128,64]{2,1,0:T(8,128)S(1)}, u32[]{:S(2)}, u32[]{:S(2)}) collective-permute-start(f32[4,128,64]{2,1,0:T(8,128)S(1)} %multiply_add_fusion.3), channel_id=1, source_target_pairs={{0,32},{32,64},{64,96},{96,128},{128,160},{160,192},{192,224},{224... | collective-permute-start | bytes 393224 | tf_op jit(solution)/shard_map/while/body/eval_jaxpr/ppermute | solution.py:14
  687.5 14.3 %collective-permute-start = (f32[4,128,64]{2,1,0:T(8,128)S(1)}, f32[4,128,64]{2,1,0:T(8,128)S(1)}, u32[]{:S(2)}, u32[]{:S(2)}) collective-permute-start(f32[4,128,64]{2,1,0:T(8,128)S(1)} %multiply_add_fusion.3), channel_id=1, source_target_pairs={{0,32},{32,64},{64,96},{96,128},{128,160},{160,192},{192,224},{224... | collective-permute-start | bytes 393224 | tf_op jit(solution)/shard_map/while/body/eval_jaxpr/ppermute | solution.py:14
  701.8 3.7 copy-start.3
  702.9 5.1 copy-start.1
  (6 other events, 10.0 us)
Sparse Core Ops, SparseCore 0:
  10.5 107.0 all-gather.7
  119.8 67.7 all-gather.5
  190.7 102.3 all-gather.11
  296.1 99.3 all-gather.9
where the time goes:
time: 722 us; the launch traced here: 721 us
  waiting for transfers between devices  527 us (73%)
  blocking collectives  56 us (8%)
  starting transfers between devices  33 us (5%)
  matrix products  31.8 us (4%)
  local copies, waits for them, and re-layouts  28.9 us (4%)
  other arithmetic  25.4 us (4%)
  between operations  13.3 us (2%)
    ppermute x16, waiting for transfers between devices, passed_along(): lax.ppermute(value, axis, [(source, source + steps) for source in range(l...  216 us
    all_gather x1, waiting for transfers between devices, local(): lax.all_gather(state_own, 'seq', axis=0, tiled=True)  98.4 us
    all_gather x1, waiting for transfers between devices, local(): lax.all_gather(gate_weight, 'seq', axis=0, tiled=True)  92.2 us
    all_gather x1, waiting for transfers between devices, local(): gathered = lax.all_gather(tokens, 'head', axis=0, tiled=True)  69.9 us
    all_gather x1, blocking collectives, local(): lax.all_gather(step_weight, 'seq', axis=0, tiled=True)  56 us
    all_gather x1, waiting for transfers between devices, local(): lax.all_gather(value_weight, 'seq', axis=0, tiled=True)  48 us
    ppermute x16, starting transfers between devices, passed_along(): lax.ppermute(value, axis, [(source, source + steps) for source in range(l...  32.9 us
    dot_general x4, matrix products, local(): jnp.dot(gathered, weight_piece, preferred_element_type=jnp.float32)  25.7 us
  transfers between devices with their start and end apart: 20, of which 19 were waited for; matrix products, arithmetic and copies ran while one was open for 5% of the time, Pallas kernels for 0%

commit v1 on v0

--- a/solution.py
+++ b/solution.py
@@ -129,7 +129,9 @@
     group_index = lax.axis_index("head") * heads_here // (HEADS // GROUPS)
     state_own = lax.dynamic_index_in_dim(state_weight, group_index, 0, keepdims=False)
     conv_own = lax.dynamic_index_in_dim(state_conv, group_index, 0, keepdims=False)
-    gathered = lax.all_gather(tokens, "head", axis=0, tiled=True)
+    gathered = jnp.concatenate(
+        lax.all_to_all(jnp.stack([tokens] * lax.axis_size("head")), "head", 0, 0), axis=0
+    )
     shard_pieces = (
         lax.all_gather(value_weight, "seq", axis=0, tiled=True),
         lax.all_gather(gate_weight, "seq", axis=0, tiled=True),

time: 722 us -> 700 us (0.970)
  waiting for transfers between devices: 527 us -> 384 us
  blocking collectives: 56 us -> 160 us
  local copies, waits for them, and re-layouts: 28.9 us -> 37.9 us
    all_gather x1, blocking collectives: 56 us -> 160 us  [local(): lax.all_gather(step_weight, 'seq', axis=0, tiled=True)]
    all_gather x1, waiting for transfers between devices: 98.4 us -> 0.01 us  [local(): lax.all_gather(state_own, 'seq', axis=0, tiled=True)]
    all_gather x1 -> x0, waiting for transfers between devices: 69.9 us -> none  [local(): gathered = lax.all_gather(tokens, 'head', axis=0, tiled=True)]
    all_to_all x0 -> x1, waiting for transfers between devices: none -> 68.6 us  [local(): lax.all_to_all(jnp.stack([tokens] * lax.axis_size('head')), 'head', 0, 0)]
    all_gather x1, waiting for transfers between devices: 48 us -> 4.51 us  [local(): lax.all_gather(value_weight, 'seq', axis=0, tiled=True)]
  transfers between devices with their start and end apart: 20 -> 20, of which waited for: 19 -> 18; matrix products, arithmetic and copies ran while one was open for 5% -> 4% of each run, Pallas kernels for 0% -> 0%
where the time goes in v1:
time: 700 us; the launch traced here: 699 us
  waiting for transfers between devices  384 us (55%)
  blocking collectives  160 us (23%)
  starting transfers between devices  39.1 us (6%)
  local copies, waits for them, and re-layouts  37.9 us (5%)
  matrix products  32.3 us (5%)
  other arithmetic  27.2 us (4%)
  between operations  13.4 us (2%)
    ppermute x16, waiting for transfers between devices, passed_along(): lax.ppermute(value, axis, [(source, source + steps) for source in range(l...  216 us
    all_gather x1, blocking collectives, local(): lax.all_gather(step_weight, 'seq', axis=0, tiled=True)  160 us
    all_gather x1, waiting for transfers between devices, local(): lax.all_gather(gate_weight, 'seq', axis=0, tiled=True)  93.2 us
    all_to_all x1, waiting for transfers between devices, local(): lax.all_to_all(jnp.stack([tokens] * lax.axis_size('head')), 'head', 0, 0)  68.6 us
    ppermute x16, starting transfers between devices, passed_along(): lax.ppermute(value, axis, [(source, source + steps) for source in range(l...  31.8 us
    dot_general x4, matrix products, local(): jnp.dot(gathered, weight_piece, preferred_element_type=jnp.float32)  25.6 us
  transfers between devices with their start and end apart: 20, of which 18 were waited for; matrix products, arithmetic and copies ran while one was open for 4% of the time, Pallas kernels for 0%

profile of v1, /device:TPU:48, one launch (start us, length us, event | category | flops | bytes accessed | tf_op | source)
XLA Modules:
  0.0 699.1 jit_solution(10771718953232695658)
XLA Ops:
  11.9 7.1 %all-to-all-start = ((bf16[32,32,4096]{2,1,0:T(8,128)(2,1)}), bf16[32,32,4096]{2,1,0:T(8,128)(2,1)}, u32[]{:S(2)}, u32[]{:S(2)}) async-start(bf16[32,32,4096]{2,1,0:T(8,128)(2,1)} %stack.2), calls=%async_computation | async-start | bytes 16777216 | tf_op jit(solution)/shard_map/all_to_all | solution.py:133
  21.9 159.7 %all_gather.14 = bf16[4096,4]{0,1:T(4,128)(2,1)S(1)} all-gather(bf16[256,4]{0,1:T(4,128)(2,1)S(1)} %copy-done.6), channel_id=1, replica_groups=mesh['seq'=16,'head'=32] {'seq'}, dimensions={0}, use_global_device_ids=true | all-gather | bytes 34816 | tf_op jit(solution)/shard_map/all_gather | solution.py:139
  182.5 68.6 %all-to-all-done = bf16[32,32,4096]{2,1,0:T(8,128)(2,1)} async-done(((bf16[32,32,4096]{2,1,0:T(8,128)(2,1)}), bf16[32,32,4096]{2,1,0:T(8,128)(2,1)}, u32[]{:S(2)}, u32[]{:S(2)}) %all-to-all-start) | async-done | bytes 8388640 | tf_op jit(solution)/shard_map/all_to_all | solution.py:133
  251.1 6.3 fusion.29
  272.0 93.2 %all-gather.7.cloned.1.call-done = bf16[4096,256]{1,0:T(8,128)(2,1)} async-done(((bf16[256,256]{1,0:T(8,128)(2,1)}), bf16[4096,256]{1,0:T(8,128)(2,1)}) %all-gather.7.cloned.1.call-update) | async-done | bytes 2097168 | tf_op jit(solution)/shard_map/all_gather | solution.py:137
  365.1 7.3 %convert_multiply_fusion = f32[1024,256]{1,0:T(8,128)} fusion(bf16[1024,4096]{1,0:T(8,128)(2,1)} %bitcast.19, bf16[4096,256]{1,0:T(8,128)(2,1)} %all-gather.7.cloned.1.call-done), kind=kOutput, calls=%fused_computation.49 | convolution fusion | flops 2149056512 | bytes 11534336 | tf_op jit(solution)/shard_map/dot_general | solution.py:143
  391.9 36.7 %while.43 = (s32[]{:T(128)}, f32[4,256,256]{1,2,0:T(8,128)}, f32[4,4,128,64]{2,3,1,0:T(8,128)}, f32[4,4]{1,0:T(4,128)S(1)}, f32[4,4,256]{2,1,0:T(4,128)S(1)}, /*...) while((s32[]{:T(128)}, f32[4,256,256]{1,2,0:T(8,128)}, ...), condition=%wide.region_5.6_spmd, body=%wide.region_2.5_spmd.sunk | while | flops 69210640 | bytes 2915319 | solution.py:75
  428.6 7.8 %while.45 = (s32[]{:T(128)}, f32[4,128,64]{2,1,0:T(8,128)S(1)}, f32[4]{0:T(128)S(1)}, f32[4,4,128,64]{3,2,1,0:T(8,128)}, f32[4,4]{1,0:T(4,128)S(1)}, /*index=5*/...) while((s32[]{:T(128)}, f32[4,128,64]{2,1,0:T(8,128)S(1)}, f32[4]{0:T(128)S(1)}, ...), condition=%wide.region_7.8_spmd.clone, body=%wide.region_6.7_spmd.clone.sunk | while | flops 131083 | bytes 1310977 | solution.py:93
  436.4 247.5 %while.44 = (s32[]{:T(128)}, f32[4,128,64]{2,1,0:T(8,128)S(1)}, f32[4]{0:T(128)S(1)}, f32[4,128,64]{2,1,0:T(8,128)S(1)}, s32[]{:T(128)}) while((s32[]{:T(128)}, f32[4,128,64]{2,1,0:T(8,128)S(1)}, f32[4]{0:T(128)S(1)}, f32[4,128,64]{2,1,0:T(8,128)S(1)}, s32[]{:T(128)}) %tuple.85), condition=%wide.region_9.10_spmd, body=%wide.region_8.9_spmd.sunk | while | flops 65538 | bytes 917621 | solution.py:176
  439.4 12.6 %collective-permute-done = f32[4,128,64]{2,1,0:T(8,128)S(1)} collective-permute-done((f32[4,128,64]{2,1,0:T(8,128)S(1)}, f32[4,128,64]{2,1,0:T(8,128)S(1)}, u32[]{:S(2)}, u32[]{:S(2)}) %collective-permute-start) | collective-permute-done | bytes 131104 | tf_op jit(solution)/shard_map/while/body/eval_jaxpr/ppermute | solution.py:14
  454.0 15.3 %collective-permute-done = f32[4,128,64]{2,1,0:T(8,128)S(1)} collective-permute-done((f32[4,128,64]{2,1,0:T(8,128)S(1)}, f32[4,128,64]{2,1,0:T(8,128)S(1)}, u32[]{:S(2)}, u32[]{:S(2)}) %collective-permute-start) | collective-permute-done | bytes 131104 | tf_op jit(solution)/shard_map/while/body/eval_jaxpr/ppermute | solution.py:14
  471.3 15.1 %collective-permute-done = f32[4,128,64]{2,1,0:T(8,128)S(1)} collective-permute-done((f32[4,128,64]{2,1,0:T(8,128)S(1)}, f32[4,128,64]{2,1,0:T(8,128)S(1)}, u32[]{:S(2)}, u32[]{:S(2)}) %collective-permute-start) | collective-permute-done | bytes 131104 | tf_op jit(solution)/shard_map/while/body/eval_jaxpr/ppermute | solution.py:14
  488.4 15.1 %collective-permute-done = f32[4,128,64]{2,1,0:T(8,128)S(1)} collective-permute-done((f32[4,128,64]{2,1,0:T(8,128)S(1)}, f32[4,128,64]{2,1,0:T(8,128)S(1)}, u32[]{:S(2)}, u32[]{:S(2)}) %collective-permute-start) | collective-permute-done | bytes 131104 | tf_op jit(solution)/shard_map/while/body/eval_jaxpr/ppermute | solution.py:14
  505.5 19.9 %collective-permute-done = f32[4,128,64]{2,1,0:T(8,128)S(1)} collective-permute-done((f32[4,128,64]{2,1,0:T(8,128)S(1)}, f32[4,128,64]{2,1,0:T(8,128)S(1)}, u32[]{:S(2)}, u32[]{:S(2)}) %collective-permute-start) | collective-permute-done | bytes 131104 | tf_op jit(solution)/shard_map/while/body/eval_jaxpr/ppermute | solution.py:14
  527.4 17.7 %collective-permute-done = f32[4,128,64]{2,1,0:T(8,128)S(1)} collective-permute-done((f32[4,128,64]{2,1,0:T(8,128)S(1)}, f32[4,128,64]{2,1,0:T(8,128)S(1)}, u32[]{:S(2)}, u32[]{:S(2)}) %collective-permute-start) | collective-permute-done | bytes 131104 | tf_op jit(solution)/shard_map/while/body/eval_jaxpr/ppermute | solution.py:14
  547.1 15.2 %collective-permute-done = f32[4,128,64]{2,1,0:T(8,128)S(1)} collective-permute-done((f32[4,128,64]{2,1,0:T(8,128)S(1)}, f32[4,128,64]{2,1,0:T(8,128)S(1)}, u32[]{:S(2)}, u32[]{:S(2)}) %collective-permute-start) | collective-permute-done | bytes 131104 | tf_op jit(solution)/shard_map/while/body/eval_jaxpr/ppermute | solution.py:14
  564.3 14.3 %collective-permute-done = f32[4,128,64]{2,1,0:T(8,128)S(1)} collective-permute-done((f32[4,128,64]{2,1,0:T(8,128)S(1)}, f32[4,128,64]{2,1,0:T(8,128)S(1)}, u32[]{:S(2)}, u32[]{:S(2)}) %collective-permute-start) | collective-permute-done | bytes 131104 | tf_op jit(solution)/shard_map/while/body/eval_jaxpr/ppermute | solution.py:14
  580.6 16.3 %collective-permute-done = f32[4,128,64]{2,1,0:T(8,128)S(1)} collective-permute-done((f32[4,128,64]{2,1,0:T(8,128)S(1)}, f32[4,128,64]{2,1,0:T(8,128)S(1)}, u32[]{:S(2)}, u32[]{:S(2)}) %collective-permute-start) | collective-permute-done | bytes 131104 | tf_op jit(solution)/shard_map/while/body/eval_jaxpr/ppermute | solution.py:14
  598.9 13.1 %collective-permute-done = f32[4,128,64]{2,1,0:T(8,128)S(1)} collective-permute-done((f32[4,128,64]{2,1,0:T(8,128)S(1)}, f32[4,128,64]{2,1,0:T(8,128)S(1)}, u32[]{:S(2)}, u32[]{:S(2)}) %collective-permute-start) | collective-permute-done | bytes 131104 | tf_op jit(solution)/shard_map/while/body/eval_jaxpr/ppermute | solution.py:14
  614.1 12.4 %collective-permute-done = f32[4,128,64]{2,1,0:T(8,128)S(1)} collective-permute-done((f32[4,128,64]{2,1,0:T(8,128)S(1)}, f32[4,128,64]{2,1,0:T(8,128)S(1)}, u32[]{:S(2)}, u32[]{:S(2)}) %collective-permute-start) | collective-permute-done | bytes 131104 | tf_op jit(solution)/shard_map/while/body/eval_jaxpr/ppermute | solution.py:14
  628.5 12.4 %collective-permute-done = f32[4,128,64]{2,1,0:T(8,128)S(1)} collective-permute-done((f32[4,128,64]{2,1,0:T(8,128)S(1)}, f32[4,128,64]{2,1,0:T(8,128)S(1)}, u32[]{:S(2)}, u32[]{:S(2)}) %collective-permute-start) | collective-permute-done | bytes 131104 | tf_op jit(solution)/shard_map/while/body/eval_jaxpr/ppermute | solution.py:14
  642.8 12.4 %collective-permute-done = f32[4,128,64]{2,1,0:T(8,128)S(1)} collective-permute-done((f32[4,128,64]{2,1,0:T(8,128)S(1)}, f32[4,128,64]{2,1,0:T(8,128)S(1)}, u32[]{:S(2)}, u32[]{:S(2)}) %collective-permute-start) | collective-permute-done | bytes 131104 | tf_op jit(solution)/shard_map/while/body/eval_jaxpr/ppermute | solution.py:14
  657.2 12.4 %collective-permute-done = f32[4,128,64]{2,1,0:T(8,128)S(1)} collective-permute-done((f32[4,128,64]{2,1,0:T(8,128)S(1)}, f32[4,128,64]{2,1,0:T(8,128)S(1)}, u32[]{:S(2)}, u32[]{:S(2)}) %collective-permute-start) | collective-permute-done | bytes 131104 | tf_op jit(solution)/shard_map/while/body/eval_jaxpr/ppermute | solution.py:14
  671.6 12.4 %collective-permute-done = f32[4,128,64]{2,1,0:T(8,128)S(1)} collective-permute-done((f32[4,128,64]{2,1,0:T(8,128)S(1)}, f32[4,128,64]{2,1,0:T(8,128)S(1)}, u32[]{:S(2)}, u32[]{:S(2)}) %collective-permute-start) | collective-permute-done | bytes 131104 | tf_op jit(solution)/shard_map/while/body/eval_jaxpr/ppermute | solution.py:14
  (238 shorter events, 121.7 us)
Async XLA Ops:
  11.9 170.5 %copy-start.8 = (f32[4]{0:T(128)S(1)}, f32[4]{0:T(128)}, u32[]{:S(2)}) copy-start(f32[4]{0:T(128)} %param.25) | copy-start | bytes 52
  11.9 170.6 %copy-start.5 = (f32[4,256]{1,0:T(4,128)S(1)}, f32[4,256]{1,0:T(4,128)}, u32[]{:S(2)}) copy-start(f32[4,256]{1,0:T(4,128)} %param.22) | copy-start | bytes 12292
  11.9 239.2 %all-to-all-start = ((bf16[32,32,4096]{2,1,0:T(8,128)(2,1)}), bf16[32,32,4096]{2,1,0:T(8,128)(2,1)}, u32[]{:S(2)}, u32[]{:S(2)}) async-start(bf16[32,32,4096]{2,1,0:T(8,128)(2,1)} %stack.2), calls=%async_computation | async-start | bytes 16777216 | tf_op jit(solution)/shard_map/all_to_all | solution.py:133
  19.0 163.5 %all-gather.9.cloned.1.call-start = ((), (), s32[]{:S(2)}) async-start(), calls=%async_computation.3 | async-start | bytes 2228224 | tf_op jit(solution)/shard_map/all_gather | solution.py:138
  19.8 242.9 %all-gather.5.cloned.1.call-start = ((), (), s32[]{:S(2)}) async-start(), calls=%async_computation.1 | async-start | bytes 2228224 | tf_op jit(solution)/shard_map/all_gather | solution.py:136
  20.5 344.6 %all-gather.7.cloned.1.call-start = ((), (), s32[]{:S(2)}) async-start(), calls=%async_computation.2 | async-start | bytes 2228224 | tf_op jit(solution)/shard_map/all_gather | solution.py:137
  269.8 102.6 %copy-start.4 = (f32[4]{0:T(128)S(1)}, f32[4]{0:T(128)}, u32[]{:S(2)}) copy-start(f32[4]{0:T(128)} %param.24) | copy-start | bytes 52
  269.9 112.0 %collective-permute-start.1 = (bf16[3,512]{1,0:T(4,128)(2,1)S(1)}, bf16[3,512]{1,0:T(4,128)(2,1)S(1)}, u32[]{:S(2)}, u32[]{:S(2)}) collective-permute-start(bf16[3,512]{1,0:T(4,128)(2,1)S(1)} %pad_maximum_fusion.2), channel_id=1, source_target_pairs={{0,32},{32,64},{64,96},{96,128},{128,160},{160,192},{192,224},{224... | collective-permute-start | bytes 9224 | tf_op jit(solution)/shard_map/ppermute | solution.py:14
  428.6 259.8 %copy-start.1 = (f32[4,256,4,64]{1,3,2,0:T(8,128)S(1)}, f32[4,256,4,64]{1,3,2,0:T(8,128)}, u32[]{:S(2)}) copy-start(f32[4,256,4,64]{1,3,2,0:T(8,128)} %copy.55) | copy-start | bytes 3145732
  436.6 15.4 %collective-permute-start = (f32[4,128,64]{2,1,0:T(8,128)S(1)}, f32[4,128,64]{2,1,0:T(8,128)S(1)}, u32[]{:S(2)}, u32[]{:S(2)}) collective-permute-start(f32[4,128,64]{2,1,0:T(8,128)S(1)} %multiply_add_fusion.3), channel_id=1, source_target_pairs={{0,32},{32,64},{64,96},{96,128},{128,160},{160,192},{192,224},{224... | collective-permute-start | bytes 393224 | tf_op jit(solution)/shard_map/while/body/eval_jaxpr/ppermute | solution.py:14
  452.1 17.2 %collective-permute-start = (f32[4,128,64]{2,1,0:T(8,128)S(1)}, f32[4,128,64]{2,1,0:T(8,128)S(1)}, u32[]{:S(2)}, u32[]{:S(2)}) collective-permute-start(f32[4,128,64]{2,1,0:T(8,128)S(1)} %multiply_add_fusion.3), channel_id=1, source_target_pairs={{0,32},{32,64},{64,96},{96,128},{128,160},{160,192},{192,224},{224... | collective-permute-start | bytes 393224 | tf_op jit(solution)/shard_map/while/body/eval_jaxpr/ppermute | solution.py:14
  469.4 17.0 %collective-permute-start = (f32[4,128,64]{2,1,0:T(8,128)S(1)}, f32[4,128,64]{2,1,0:T(8,128)S(1)}, u32[]{:S(2)}, u32[]{:S(2)}) collective-permute-start(f32[4,128,64]{2,1,0:T(8,128)S(1)} %multiply_add_fusion.3), channel_id=1, source_target_pairs={{0,32},{32,64},{64,96},{96,128},{128,160},{160,192},{192,224},{224... | collective-permute-start | bytes 393224 | tf_op jit(solution)/shard_map/while/body/eval_jaxpr/ppermute | solution.py:14
  486.5 17.0 %collective-permute-start = (f32[4,128,64]{2,1,0:T(8,128)S(1)}, f32[4,128,64]{2,1,0:T(8,128)S(1)}, u32[]{:S(2)}, u32[]{:S(2)}) collective-permute-start(f32[4,128,64]{2,1,0:T(8,128)S(1)} %multiply_add_fusion.3), channel_id=1, source_target_pairs={{0,32},{32,64},{64,96},{96,128},{128,160},{160,192},{192,224},{224... | collective-permute-start | bytes 393224 | tf_op jit(solution)/shard_map/while/body/eval_jaxpr/ppermute | solution.py:14
  503.6 21.8 %collective-permute-start = (f32[4,128,64]{2,1,0:T(8,128)S(1)}, f32[4,128,64]{2,1,0:T(8,128)S(1)}, u32[]{:S(2)}, u32[]{:S(2)}) collective-permute-start(f32[4,128,64]{2,1,0:T(8,128)S(1)} %multiply_add_fusion.3), channel_id=1, source_target_pairs={{0,32},{32,64},{64,96},{96,128},{128,160},{160,192},{192,224},{224... | collective-permute-start | bytes 393224 | tf_op jit(solution)/shard_map/while/body/eval_jaxpr/ppermute | solution.py:14
  525.5 19.6 %collective-permute-start = (f32[4,128,64]{2,1,0:T(8,128)S(1)}, f32[4,128,64]{2,1,0:T(8,128)S(1)}, u32[]{:S(2)}, u32[]{:S(2)}) collective-permute-start(f32[4,128,64]{2,1,0:T(8,128)S(1)} %multiply_add_fusion.3), channel_id=1, source_target_pairs={{0,32},{32,64},{64,96},{96,128},{128,160},{160,192},{192,224},{224... | collective-permute-start | bytes 393224 | tf_op jit(solution)/shard_map/while/body/eval_jaxpr/ppermute | solution.py:14
  545.2 17.1 %collective-permute-start = (f32[4,128,64]{2,1,0:T(8,128)S(1)}, f32[4,128,64]{2,1,0:T(8,128)S(1)}, u32[]{:S(2)}, u32[]{:S(2)}) collective-permute-start(f32[4,128,64]{2,1,0:T(8,128)S(1)} %multiply_add_fusion.3), channel_id=1, source_target_pairs={{0,32},{32,64},{64,96},{96,128},{128,160},{160,192},{192,224},{224... | collective-permute-start | bytes 393224 | tf_op jit(solution)/shard_map/while/body/eval_jaxpr/ppermute | solution.py:14
  562.4 16.2 %collective-permute-start = (f32[4,128,64]{2,1,0:T(8,128)S(1)}, f32[4,128,64]{2,1,0:T(8,128)S(1)}, u32[]{:S(2)}, u32[]{:S(2)}) collective-permute-start(f32[4,128,64]{2,1,0:T(8,128)S(1)} %multiply_add_fusion.3), channel_id=1, source_target_pairs={{0,32},{32,64},{64,96},{96,128},{128,160},{160,192},{192,224},{224... | collective-permute-start | bytes 393224 | tf_op jit(solution)/shard_map/while/body/eval_jaxpr/ppermute | solution.py:14
  578.7 18.2 %collective-permute-start = (f32[4,128,64]{2,1,0:T(8,128)S(1)}, f32[4,128,64]{2,1,0:T(8,128)S(1)}, u32[]{:S(2)}, u32[]{:S(2)}) collective-permute-start(f32[4,128,64]{2,1,0:T(8,128)S(1)} %multiply_add_fusion.3), channel_id=1, source_target_pairs={{0,32},{32,64},{64,96},{96,128},{128,160},{160,192},{192,224},{224... | collective-permute-start | bytes 393224 | tf_op jit(solution)/shard_map/while/body/eval_jaxpr/ppermute | solution.py:14
  597.0 15.0 %collective-permute-start = (f32[4,128,64]{2,1,0:T(8,128)S(1)}, f32[4,128,64]{2,1,0:T(8,128)S(1)}, u32[]{:S(2)}, u32[]{:S(2)}) collective-permute-start(f32[4,128,64]{2,1,0:T(8,128)S(1)} %multiply_add_fusion.3), channel_id=1, source_target_pairs={{0,32},{32,64},{64,96},{96,128},{128,160},{160,192},{192,224},{224... | collective-permute-start | bytes 393224 | tf_op jit(solution)/shard_map/while/body/eval_jaxpr/ppermute | solution.py:14
  612.1 14.3 %collective-permute-start = (f32[4,128,64]{2,1,0:T(8,128)S(1)}, f32[4,128,64]{2,1,0:T(8,128)S(1)}, u32[]{:S(2)}, u32[]{:S(2)}) collective-permute-start(f32[4,128,64]{2,1,0:T(8,128)S(1)} %multiply_add_fusion.3), channel_id=1, source_target_pairs={{0,32},{32,64},{64,96},{96,128},{128,160},{160,192},{192,224},{224... | collective-permute-start | bytes 393224 | tf_op jit(solution)/shard_map/while/body/eval_jaxpr/ppermute | solution.py:14
  626.5 14.3 %collective-permute-start = (f32[4,128,64]{2,1,0:T(8,128)S(1)}, f32[4,128,64]{2,1,0:T(8,128)S(1)}, u32[]{:S(2)}, u32[]{:S(2)}) collective-permute-start(f32[4,128,64]{2,1,0:T(8,128)S(1)} %multiply_add_fusion.3), channel_id=1, source_target_pairs={{0,32},{32,64},{64,96},{96,128},{128,160},{160,192},{192,224},{224... | collective-permute-start | bytes 393224 | tf_op jit(solution)/shard_map/while/body/eval_jaxpr/ppermute | solution.py:14
  640.9 14.3 %collective-permute-start = (f32[4,128,64]{2,1,0:T(8,128)S(1)}, f32[4,128,64]{2,1,0:T(8,128)S(1)}, u32[]{:S(2)}, u32[]{:S(2)}) collective-permute-start(f32[4,128,64]{2,1,0:T(8,128)S(1)} %multiply_add_fusion.3), channel_id=1, source_target_pairs={{0,32},{32,64},{64,96},{96,128},{128,160},{160,192},{192,224},{224... | collective-permute-start | bytes 393224 | tf_op jit(solution)/shard_map/while/body/eval_jaxpr/ppermute | solution.py:14
  655.3 14.3 %collective-permute-start = (f32[4,128,64]{2,1,0:T(8,128)S(1)}, f32[4,128,64]{2,1,0:T(8,128)S(1)}, u32[]{:S(2)}, u32[]{:S(2)}) collective-permute-start(f32[4,128,64]{2,1,0:T(8,128)S(1)} %multiply_add_fusion.3), channel_id=1, source_target_pairs={{0,32},{32,64},{64,96},{96,128},{128,160},{160,192},{192,224},{224... | collective-permute-start | bytes 393224 | tf_op jit(solution)/shard_map/while/body/eval_jaxpr/ppermute | solution.py:14
  669.7 14.3 %collective-permute-start = (f32[4,128,64]{2,1,0:T(8,128)S(1)}, f32[4,128,64]{2,1,0:T(8,128)S(1)}, u32[]{:S(2)}, u32[]{:S(2)}) collective-permute-start(f32[4,128,64]{2,1,0:T(8,128)S(1)} %multiply_add_fusion.3), channel_id=1, source_target_pairs={{0,32},{32,64},{64,96},{96,128},{128,160},{160,192},{192,224},{224... | collective-permute-start | bytes 393224 | tf_op jit(solution)/shard_map/while/body/eval_jaxpr/ppermute | solution.py:14
  (5 other events, 33.6 us)
Sparse Core Ops, SparseCore 0:
  23.0 129.9 all-gather.8
  156.2 106.4 all-gather.4
  265.9 99.1 all-gather.6
